TPU v7x, 256 devices: a whole 4x4x8 slice. The times are simulated.
256 devices in a mesh: dp: 32 (over y, x, core), tensor: 8 (over z).
Axes of the slice: x: 4, y: 4, z: 8, core: 2. Of those that a mesh axis runs over, the one named last changes fastest.
Arguments:
- patches: bfloat16 [16384, 1280], P('dp'), may hold values from -6 to 6
- window_ids: int32 [32, 512], P('dp'), may hold values from 0 to 15, never falling along the last dimension, each value on 1 to 64 neighbouring positions
- vit_gain: float32 [1280], replicated, may hold values from 0.5 to 2
- qkv_weight: bfloat16 [3, 1280, 1280], P(None, None, 'tensor'), may hold values from -0.15625 to 0.15625
- out_weight: bfloat16 [1280, 1280], P('tensor'), may hold values from -0.15625 to 0.15625
- merge_gain: float32 [1280], replicated, may hold values from 0.5 to 2
- merger_weight: bfloat16 [5120, 3584], P(None, 'tensor'), may hold values from -0.078125 to 0.078125
- audio: bfloat16 [12288, 3584], P('dp', 'tensor'), may hold values from -6 to 6
- span_lengths: int32 [32, 32], replicated, may hold values from 8 to 32, as said below
- span_time: int32 [32, 32], replicated, may hold values from 0 to 31, each once within a row
- llm_gain: float32 [3584], replicated, may hold values from 0.5 to 2
- gate_weight: bfloat16 [3584, 9472], P('dp', 'tensor'), may hold values from -0.09375 to 0.09375
- up_weight: bfloat16 [3584, 9472], P('dp', 'tensor'), may hold values from -0.09375 to 0.09375
- down_weight: bfloat16 [9472, 3584], P('tensor', 'dp'), may hold values from -0.0625 to 0.0625
Outputs:
- mixed: bfloat16 [16384, 3584], P(('dp', 'tensor'))
Inputs may be any that keep to these rules, and one draw needn't show every extreme that they name: `span_lengths`: every row and every column sums to 512; every row and every column holds the value 32 at least once. `span_time`: each row is a permutation of the owners' numbers. `window_ids`: window numbers never fall along a row; a window holds at most 64 patches.
All inputs are finite; a program needn't handle non-finite values.
Results may differ from a plain program's by a relative error of at most 0.017.
Values may be sent and summed in bfloat16 or wider, within the bound.
No kernel may reach another device: no remote copies, remote signals or barrier semaphores. Data moves between devices by JAX's collectives and lax.ppermute only.
A program may use at most 128 MiB of HBM per device.

v0:
```python
import math
import jax
import jax.numpy as jnp
from jax import lax
from jax.sharding import PartitionSpec as P

D_VIT = 1280
HEAD_VIT = 80
EPSILON = 1e-06


def in_blocks(x, dim, devices):
    before, after = (x.shape[:dim], x.shape[dim + 1 :])
    return jnp.moveaxis(x.reshape(*before, devices, -1, *after), dim, 0)


def sent_and_summed(x, axis, dim):
    parts = in_blocks(x, dim, lax.axis_size(axis))
    arrived = lax.all_to_all(parts, axis, split_axis=0, concat_axis=0, tiled=True)
    return arrived.astype(jnp.float32).sum(axis=0)


def from_everyone(x, axis):
    devices = lax.axis_size(axis)
    return lax.all_to_all(jnp.broadcast_to(x[None], (devices, *x.shape)), axis, 0, 0, tiled=True)


def in_order(parts, dim):
    parts = jnp.moveaxis(parts, 0, dim)
    dims = parts.shape
    return parts.reshape(*dims[:dim], dims[dim] * dims[dim + 1], *dims[dim + 2 :])


def gather_directly(x, axis, dim):
    parts = from_everyone(x, axis)
    return in_order(parts, dim)


def gather_turned(arrays, axis, dims):
    turned = [jnp.moveaxis(a, dim, 0) for a, dim in zip(arrays, dims)]
    widths = [t[0].size for t in turned]
    both = jnp.concatenate([t.reshape(-1, w) for t, w in zip(turned, widths)], axis=1)
    whole = lax.all_gather(both, axis, axis=0, tiled=True)
    parts = jnp.split(whole, [sum(widths[:k]) for k in range(1, len(widths))], axis=1)
    return tuple(
        (
            jnp.moveaxis(b.reshape(-1, *t.shape[1:]), 0, dim)
            for b, t, dim in zip(parts, turned, dims)
        )
    )


def rms_scale(values, gain):
    wide = values.astype(jnp.float32)
    meansq = jnp.mean(wide * wide, axis=-1, keepdims=True)
    return wide * lax.rsqrt(meansq + EPSILON) * gain


def body(
    patches,
    window_ids,
    vit_gain,
    qkv_weight,
    out_weight,
    merge_gain,
    merger_weight,
    audio,
    span_lengths,
    span_time,
    llm_gain,
    gate_weight,
    up_weight,
    down_weight,
):
    patch_count = patches.shape[0]
    heads_here = qkv_weight.shape[2] // HEAD_VIT
    normed = rms_scale(patches, vit_gain).astype(jnp.bfloat16)
    query = jnp.dot(normed, qkv_weight[0], preferred_element_type=jnp.float32).astype(jnp.bfloat16)
    keys = jnp.dot(normed, qkv_weight[1], preferred_element_type=jnp.float32).astype(jnp.bfloat16)
    values = jnp.dot(normed, qkv_weight[2], preferred_element_type=jnp.float32).astype(jnp.bfloat16)
    query = query.reshape(patch_count, heads_here, HEAD_VIT)
    keys = keys.reshape(patch_count, heads_here, HEAD_VIT)
    values = values.reshape(patch_count, heads_here, HEAD_VIT)
    scores = jnp.einsum(
        "phe,qhe->hpq", query, keys, preferred_element_type=jnp.float32
    ) / math.sqrt(HEAD_VIT)
    windows = window_ids[0]
    same = windows[:, None] == windows[None, :]
    scores = jnp.where(same[None], scores, -1e30)
    probs = jax.nn.softmax(scores, axis=-1).astype(jnp.bfloat16)
    context = jnp.einsum("hpq,qhe->phe", probs, values, preferred_element_type=jnp.float32).astype(
        jnp.bfloat16
    )
    context = context.reshape(patch_count, heads_here * HEAD_VIT)
    partial_value = jnp.dot(context, out_weight, preferred_element_type=jnp.float32)
    share = sent_and_summed(partial_value.astype(jnp.bfloat16), "tensor", 0)
    share_rows = share.shape[0]
    own_frames = lax.dynamic_slice_in_dim(
        patches, lax.axis_index("tensor") * share_rows, share_rows, 0
    )
    own_encoded = (own_frames.astype(jnp.float32) + share).astype(jnp.bfloat16)
    encoded = gather_directly(own_encoded, "tensor", 0)
    merged = (
        rms_scale(encoded, merge_gain).astype(jnp.bfloat16).reshape(patch_count // 4, 4 * D_VIT)
    )
    video = jnp.dot(merged, merger_weight, preferred_element_type=jnp.float32).astype(jnp.bfloat16)
    source = jnp.concatenate([video, audio], axis=0)
    seq_count = source.shape[0]
    owner_count = lax.axis_size("dp")
    owner = lax.axis_index("dp")
    capacity = 2 * seq_count // owner_count
    sent_lengths = span_lengths[owner]
    starts = jnp.cumsum(sent_lengths) - sent_lengths
    slot_index = jnp.arange(capacity, dtype=jnp.int32)
    occupied = slot_index[None, :] < sent_lengths[:, None]
    source_index = jnp.where(occupied, starts[:, None] + slot_index[None, :], 0).reshape(-1)
    outgoing = jnp.take(source, source_index, axis=0)
    outgoing = jnp.where(occupied.reshape(-1)[:, None], outgoing, jnp.zeros((), outgoing.dtype))
    incoming = lax.all_to_all(outgoing, "dp", split_axis=0, concat_axis=0, tiled=True)
    taken_lengths = span_lengths[:, owner]
    arrival = span_time[owner]
    earlier = arrival[:, None] < arrival[None, :]
    offsets = jnp.sum(jnp.where(earlier, taken_lengths[:, None], 0), axis=0)
    position = jnp.arange(seq_count, dtype=jnp.int32)
    inside = (position[None, :] >= offsets[:, None]) & (
        position[None, :] < offsets[:, None] + taken_lengths[:, None]
    )
    sender = jnp.arange(owner_count, dtype=jnp.int32)[:, None]
    slot_row = sender * capacity + position[None, :] - offsets[:, None]
    picked = jnp.sum(jnp.where(inside, slot_row, 0), axis=0)
    sequence = jnp.take(incoming, picked, axis=0)
    features = lax.all_gather(sequence, "tensor", axis=1, tiled=True)
    normed_seq = rms_scale(features, llm_gain).astype(jnp.bfloat16)
    gate_full, up_full, down_full = gather_turned(
        (gate_weight, up_weight, down_weight), "dp", (0, 0, 1)
    )
    gate = jnp.dot(normed_seq, gate_full, preferred_element_type=jnp.float32)
    upward = jnp.dot(normed_seq, up_full, preferred_element_type=jnp.float32)
    hidden = (jax.nn.silu(gate) * upward).astype(jnp.bfloat16)
    terms = jnp.dot(hidden, down_full, preferred_element_type=jnp.float32)
    summed = lax.psum_scatter(
        terms.astype(jnp.bfloat16), "tensor", scatter_dimension=0, tiled=True
    ).astype(jnp.float32)
    own_count = summed.shape[0]
    own_rows = lax.dynamic_slice_in_dim(
        features, lax.axis_index("tensor") * own_count, own_count, 0
    )
    return (own_rows.astype(jnp.float32) + summed).astype(jnp.bfloat16)


def solution(mesh):
    return jax.shard_map(
        body,
        mesh=mesh,
        in_specs=(
            P("dp", None),
            P("dp", None),
            P(),
            P(None, None, "tensor"),
            P("tensor", None),
            P(),
            P(None, "tensor"),
            P("dp", "tensor"),
            P(),
            P(),
            P(),
            P("dp", "tensor"),
            P("dp", "tensor"),
            P("tensor", "dp"),
        ),
        out_specs=P(("dp", "tensor"), None),
        check_vma=False,
    )
```

profile of v0, /device:TPU:1, one launch (start us, length us, event | category | flops | bytes accessed | tf_op | source)
XLA Modules:
  0.0 377.8 jit_solution(1047735685525039576)
XLA Ops:
  6.5 1.8 fusion.19
  8.4 2.1 convolution_convert_fusion.3
  10.5 0.0 copy-start.8
  10.5 0.7 convolution_convert_fusion.2
  11.1 0.7 convolution_convert_fusion.4
  11.8 0.0 copy-done.8
  11.8 0.2 broadcast_compare_fusion
  12.0 1.0 fusion.61
  13.0 1.2 convolution_convert_fusion.1
  14.3 1.6 convolution_convert_fusion
  15.9 9.0 %all-to-all-start = ((bf16[8,64,1280]{2,1,0:T(8,128)(2,1)}), bf16[8,64,1280]{2,1,0:T(8,128)(2,1)S(1)}, u32[]{:S(2)}, u32[]{:S(2)}) async-start(bf16[8,64,1280]{2,1,0:T(8,128)(2,1)} %bitcast.15), calls=%async_computation | async-start | bytes 2621440 | tf_op jit(solution)/shard_map/all_to_all | solution.py:19
  24.9 34.9 %all-to-all-done = bf16[8,64,1280]{2,1,0:T(8,128)(2,1)S(1)} async-done(((bf16[8,64,1280]{2,1,0:T(8,128)(2,1)}), bf16[8,64,1280]{2,1,0:T(8,128)(2,1)S(1)}, u32[]{:S(2)}, u32[]{:S(2)}) %all-to-all-start) | async-done | bytes 1310752 | tf_op jit(solution)/shard_map/all_to_all | solution.py:19
  59.8 0.2 convert_reduce_fusion
  60.0 0.0 copy-start.9
  60.0 0.0 copy-start.3
  60.0 0.0 copy-start.7
  60.1 1.1 broadcast_in_dim.103
  61.2 3.6 all-to-all-start.1
  64.8 0.2 copy.36
  65.1 0.1 copy.33
  65.2 0.1 reduce-window.8
  65.2 0.1 reduce.1
  65.3 0.1 add_select_fusion
  65.4 0.1 select_n.94
  65.5 0.1 constant_dynamic-slice_fusion.2
  65.6 0.1 copy.40
  65.7 0.7 fusion.44
  66.4 0.1 select_reduce_fusion.1
  66.5 0.1 iota_compare_fusion.2
  66.6 32.9 %all-to-all-done.1 = bf16[8,64,1280]{2,1,0:T(8,128)(2,1)S(1)} async-done(((bf16[8,64,1280]{2,1,0:T(8,128)(2,1)}), bf16[8,64,1280]{2,1,0:T(8,128)(2,1)S(1)}, u32[]{:S(2)}, u32[]{:S(2)}) %all-to-all-start.1) | async-done | bytes 1310752 | tf_op jit(solution)/shard_map/all_to_all | solution.py:25
  99.5 0.3 multiply_reduce_fusion
  99.9 0.1 rsqrt.29
  100.0 0.4 mul.97
  100.4 2.0 copy.42
  102.3 1.9 reshape.242
  104.2 5.2 %fusion.25 = bf16[128,448]{0,1:T(8,128)(2,1)S(1)} fusion(bf16[5120,448]{0,1:T(8,128)(2,1)} %param.20, f32[128,5120]{1,0:T(8,128)} %reshape.242, f32[128,5120]{1,0:T(8,128)} %bitcast.49, f32[5120]{0:T(1024)S(1)} %mul.101), kind=kOutput, calls=%fused_computation.36 | convolution fusion | flops 589225984 | bytes 9965568 | tf_op jit(solution)/shard_map/dot_general | solution.py:106
  109.4 0.1 copy.35
  109.6 0.1 pad_maximum_fusion
  109.6 4.0 %gather_fusion = bf16[1024,448]{1,0:T(8,128)(2,1)S(1)} fusion(bf16[512,448]{1,0:T(8,128)(2,1)S(1)} %pad_maximum_fusion, s32[1024]{0:T(1024)S(1)} %broadcast_clamp_fusion), kind=kCustom, calls=%fused_computation | custom fusion | bytes 1839104 | tf_op jit(solution)/shard_map/jit(_take)/gather | solution.py:117
  113.6 1.3 select_select_fusion
  114.9 7.6 %all-to-all-start.2 = ((bf16[32,32,448]{2,1,0:T(8,128)(2,1)}), bf16[32,32,448]{2,1,0:T(8,128)(2,1)S(1)}, u32[]{:S(2)}, u32[]{:S(2)}) async-start(bf16[32,32,448]{2,1,0:T(8,128)(2,1)} %select_select_fusion), calls=%async_computation.2 | async-start | bytes 2097152 | tf_op jit(solution)/shard_map/all_to_all | solution.py:119
  122.4 0.0 all-gather.3.cloned.1.call-start
  122.5 0.1 select_reduce_fusion
  122.6 17.0 %all-to-all-done.2 = bf16[32,32,448]{2,1,0:T(8,128)(2,1)S(1)} async-done(((bf16[32,32,448]{2,1,0:T(8,128)(2,1)}), bf16[32,32,448]{2,1,0:T(8,128)(2,1)S(1)}, u32[]{:S(2)}, u32[]{:S(2)}) %all-to-all-start.2) | async-done | bytes 917536 | tf_op jit(solution)/shard_map/all_to_all | solution.py:119
  139.6 2.0 gather_fusion.1
  141.6 0.1 broadcast_select_fusion
  141.7 1.0 copy.37
  142.7 0.0 all-gather.3.cloned.1.call-update
  142.7 0.0 all-gather.5.cloned.1.call-start
  142.8 1.4 concatenate.7
  144.2 0.0 all-gather.5.cloned.1.call-update
  144.2 0.2 reduce-scatter.2.cloned.1.call-start
  144.4 40.7 %all-gather.3.cloned.1.call-done = bf16[512,3584]{0,1:T(8,128)(2,1)} async-done(((bf16[512,448]{0,1:T(8,128)(2,1)}), bf16[512,3584]{0,1:T(8,128)(2,1)}) %all-gather.3.cloned.1.call-update) | async-done | bytes 3670032 | tf_op jit(solution)/shard_map/all_gather | solution.py:132
  185.1 2.9 fusion.7
  188.0 97.1 %all-gather.5.cloned.1.call-done = bf16[3584,3552]{1,0:T(8,128)(2,1)} async-done(((bf16[112,3552]{1,0:T(8,128)(2,1)}), bf16[3584,3552]{1,0:T(8,128)(2,1)}) %all-gather.5.cloned.1.call-update) | async-done | bytes 25460752 | tf_op jit(solution)/shard_map/all_gather | solution.py:43
  285.1 9.8 %fusion.5 = f32[512,1184]{0,1:T(8,128)S(1)} fusion(bf16[3584,3552]{1,0:T(8,128)(2,1)} %all-gather.5.cloned.1.call-done, bf16[512,3584]{0,1:T(8,128)(2,1)} %all-gather.3.cloned.1.call-done, f32[3584]{0:T(1024)S(1)} %copy-done.11, f32[512]{0:T(512)S(1)} %add_rsqrt_fusion.1), kind=kOutput, calls=%fused_computation.7 | convolution fusion | flops 4352638976 | bytes 15286272 | tf_op jit(solution)/shard_map/dot_general | solution.py:137
  294.9 24.9 %fusion.10 = bf16[512,3584]{1,0:T(8,128)(2,1)} fusion(bf16[3584,3552]{1,0:T(8,128)(2,1)} %all-gather.5.cloned.1.call-done, f32[512,1184]{0,1:T(8,128)S(1)} %fusion.5, bf16[512,3584]{0,1:T(8,128)(2,1)} %all-gather.3.cloned.1.call-done, f32[3584]{0:T(1024)S(1)} %copy-done.11, f32[512]{0:T(512)S(1)} %add_rsqrt_fusion.1), kind=kOutput, calls=%fused_computation.14 | convolution fusion | flops 8703410176 | bytes 28131328 | tf_op jit(solution)/shard_map/dot_general | solution.py:140
  319.8 0.0 reduce-scatter.2.cloned.1.call-update
  319.8 0.0 copy-start.1
  319.8 1.6 constant_dynamic-slice_fusion
  321.4 0.3 copy.41
  321.7 47.7 %reduce-scatter.2.cloned.1.call-done = bf16[64,3584]{1,0:T(8,128)(2,1)} async-done(((bf16[512,3584]{1,0:T(8,128)(2,1)}), bf16[64,3584]{1,0:T(8,128)(2,1)}) %reduce-scatter.2.cloned.1.call-update) | async-done | bytes 458768 | tf_op jit(solution)/shard_map/reduce_scatter | solution.py:141
  369.4 1.9 add_convert_fusion
  371.3 0.0 copy-done.1
  (34 shorter events, 0.2 us)
Async XLA Ops:
  6.5 7.7 %copy-start = (bf16[160,1280]{1,0:T(8,128)(2,1)S(1)}, bf16[160,1280]{1,0:T(8,128)(2,1)}, u32[]{:S(2)}) copy-start(bf16[160,1280]{1,0:T(8,128)(2,1)} %param.18) | copy-start | bytes 1228804
  6.5 3.9 %copy-start.2 = (bf16[512,1280]{1,0:T(8,128)(2,1)S(1)}, bf16[512,1280]{1,0:T(8,128)(2,1)}, u32[]{:S(2)}) copy-start(bf16[512,1280]{1,0:T(8,128)(2,1)} %param.14) | copy-start | bytes 3932164
  6.5 3.9 %copy-start.12 = (f32[1280]{0:T(1024)S(1)}, f32[1280]{0:T(1024)}, u32[]{:S(2)}) copy-start(f32[1280]{0:T(1024)} %param.16) | copy-start | bytes 15364
  6.5 3.9 %copy-start.10 = (bf16[3,1280,160]{1,2,0:T(8,128)(2,1)S(1)}, bf16[3,1280,160]{1,2,0:T(8,128)(2,1)}, u32[]{:S(2)}) copy-start(bf16[3,1280,160]{1,2,0:T(8,128)(2,1)} %param.17) | copy-start | bytes 3686404
  10.5 1.3 copy-start.8
  15.9 43.9 %all-to-all-start = ((bf16[8,64,1280]{2,1,0:T(8,128)(2,1)}), bf16[8,64,1280]{2,1,0:T(8,128)(2,1)S(1)}, u32[]{:S(2)}, u32[]{:S(2)}) async-start(bf16[8,64,1280]{2,1,0:T(8,128)(2,1)} %bitcast.15), calls=%async_computation | async-start | bytes 2621440 | tf_op jit(solution)/shard_map/all_to_all | solution.py:19
  60.0 4.8 %copy-start.9 = (f32[1280]{0:T(1024)S(1)}, f32[1280]{0:T(1024)}, u32[]{:S(2)}) copy-start(f32[1280]{0:T(1024)} %param.19) | copy-start | bytes 15364
  60.0 4.8 %copy-start.3 = (bf16[384,448]{0,1:T(8,128)(2,1)S(1)}, bf16[384,448]{0,1:T(8,128)(2,1)}, u32[]{:S(2)}) copy-start(bf16[384,448]{0,1:T(8,128)(2,1)} %param.21) | copy-start | bytes 1032196
  60.0 5.0 %copy-start.7 = (s32[32,32]{1,0:T(8,128)S(1)}, s32[32,32]{1,0:T(8,128)}, u32[]{:S(2)}) copy-start(s32[32,32]{1,0:T(8,128)} %param.22) | copy-start | bytes 12292
  61.2 38.3 %all-to-all-start.1 = ((bf16[8,64,1280]{2,1,0:T(8,128)(2,1)}), bf16[8,64,1280]{2,1,0:T(8,128)(2,1)S(1)}, u32[]{:S(2)}, u32[]{:S(2)}) async-start(bf16[8,64,1280]{2,1,0:T(8,128)(2,1)} %broadcast_in_dim.103), calls=%async_computation.1 | async-start | bytes 2621440 | tf_op jit(solution)/shard_map/all_to_all | solution.py:25
  114.9 24.8 %all-to-all-start.2 = ((bf16[32,32,448]{2,1,0:T(8,128)(2,1)}), bf16[32,32,448]{2,1,0:T(8,128)(2,1)S(1)}, u32[]{:S(2)}, u32[]{:S(2)}) async-start(bf16[32,32,448]{2,1,0:T(8,128)(2,1)} %select_select_fusion), calls=%async_computation.2 | async-start | bytes 2097152 | tf_op jit(solution)/shard_map/all_to_all | solution.py:119
  122.4 62.7 %all-gather.3.cloned.1.call-start = ((), (), s32[]{:S(2)}) async-start(), calls=%async_computation.4 | async-start | bytes 4128768 | tf_op jit(solution)/shard_map/all_gather | solution.py:132
  139.6 3.2 copy-start.4
  139.6 3.2 copy-start.5
  139.6 3.2 copy-start.6
  142.7 142.4 %all-gather.5.cloned.1.call-start = ((), (), s32[]{:S(2)}) async-start(), calls=%async_computation.5 | async-start | bytes 26492928 | tf_op jit(solution)/shard_map/all_gather | solution.py:43
  144.1 141.0 %copy-start.11 = (f32[3584]{0:T(1024)S(1)}, f32[3584]{0:T(1024)}, u32[]{:S(2)}) copy-start(f32[3584]{0:T(1024)} %param.24) | copy-start | bytes 43012
  144.2 225.2 %reduce-scatter.2.cloned.1.call-start = ((), (), s32[]{:S(2)}) async-start(), calls=%async_computation.6 | async-start | bytes 4128768 | tf_op jit(solution)/shard_map/reduce_scatter | solution.py:141
  319.8 51.5 %copy-start.1 = (bf16[160,1280]{1,0:T(8,128)(2,1)S(1)}, bf16[160,1280]{1,0:T(8,128)(2,1)}, u32[]{:S(2)}) copy-start(bf16[160,1280]{1,0:T(8,128)(2,1)} %param.18) | copy-start | bytes 1228804
Sparse Core Ops, SparseCore 0:
  142.8 42.2 all-gather.2
  187.7 97.3 all-gather.4
  319.9 49.4 reduce-scatter.1
where the time goes:
time: 378 us
  waiting for transfers between devices  270 us (71%)
  matrix products  47.1 us (12%)
  starting transfers between devices  20.5 us (5%)
  local copies, waits for them, and re-layouts  17 us (4%)
  between operations  13.5 us (4%)
  other arithmetic  9.35 us (2%)
    all_gather x1, waiting for transfers between devices, gather_turned(): whole = lax.all_gather(both, axis, axis=0, tiled=True)  97.1 us
    reduce_scatter x1, waiting for transfers between devices, body(): lax.psum_scatter(terms.astype(jnp.bfloat16), 'tensor', scatter_dimension=...  47.7 us
    all_gather x1, waiting for transfers between devices, body(): features = lax.all_gather(sequence, 'tensor', axis=1, tiled=True)  40.7 us
    all_to_all x1, waiting for transfers between devices, sent_and_summed(): lax.all_to_all(parts, axis, split_axis=0, concat_axis=0, tiled=True)  34.9 us
    all_to_all x1, waiting for transfers between devices, from_everyone(): lax.all_to_all(jnp.broadcast_to(x[None], (devices, *x.shape)), axis, 0, 0...  32.9 us
    dot_general x1, matrix products, body(): terms = jnp.dot(hidden, down_full, preferred_element_type=jnp.float32)  24.9 us
    all_to_all x1, waiting for transfers between devices, body(): lax.all_to_all(outgoing, 'dp', split_axis=0, concat_axis=0, tiled=True)  17 us
    dot_general x1, matrix products, body(): gate = jnp.dot(normed_seq, gate_full, preferred_element_type=jnp.float32)  9.77 us
  transfers between devices with their start and end apart: 6, of which 6 were waited for; matrix products, arithmetic and copies ran while one was open for 2% of the time, Pallas kernels for 0%

commit v1 on v0

--- a/solution.py
+++ b/solution.py
@@ -129,7 +129,14 @@
     slot_row = sender * capacity + position[None, :] - offsets[:, None]
     picked = jnp.sum(jnp.where(inside, slot_row, 0), axis=0)
     sequence = jnp.take(incoming, picked, axis=0)
-    features = lax.all_gather(sequence, "tensor", axis=1, tiled=True)
+    ring = [sequence]
+    for hop in range(7):
+        ring.append(lax.ppermute(ring[-1], "tensor", [(dev, (dev + 1) % 8) for dev in range(8)]))
+    features = jnp.roll(
+        jnp.concatenate(ring[::-1], axis=1),
+        (lax.axis_index("tensor") + 1) * ring[0].shape[1],
+        axis=1,
+    )
     normed_seq = rms_scale(features, llm_gain).astype(jnp.bfloat16)
     gate_full, up_full, down_full = gather_turned(
         (gate_weight, up_weight, down_weight), "dp", (0, 0, 1)

time: 378 us -> 349 us (0.923)
  waiting for transfers between devices: 270 us -> 221 us
  local copies, waits for them, and re-layouts: 17 us -> 27 us
  matrix products: 47.1 us -> 54.3 us
    all_gather x1, waiting for transfers between devices: 97.1 us -> 0.02 us  [gather_turned(): whole = lax.all_gather(both, axis, axis=0, tiled=True)]
    ppermute x0 -> x7, waiting for transfers between devices: none -> 83.3 us  [body(): lax.ppermute(ring[-1], 'tensor', [(dev, (dev + 1) % 8) for dev in range(8)])]
    all_gather x1 -> x0, waiting for transfers between devices: 40.7 us -> none  [body(): features = lax.all_gather(sequence, 'tensor', axis=1, tiled=True)]
    dot_general x0 -> x1, matrix products: none -> 14.2 us  [body(): upward = jnp.dot(normed_seq, up_full, preferred_element_type=jnp.float32)]
    concatenate x0 -> x1, local copies, waits for them, and re-layouts: none -> 11.6 us  [body(): jnp.roll(jnp.concatenate(ring[::-1], axis=1), (lax.axis_index('tensor') +...]
    dot_general x1, matrix products: 24.9 us -> 15.8 us  [body(): terms = jnp.dot(hidden, down_full, preferred_element_type=jnp.float32)]
    reduce_scatter x1, waiting for transfers between devices: 47.7 us -> 52.8 us  [body(): lax.psum_scatter(terms.astype(jnp.bfloat16), 'tensor', scatter_dimension=...]
  transfers between devices with their start and end apart: 6 -> 12, of which waited for: 6 -> 11; matrix products, arithmetic and copies ran while one was open for 2% -> 14% of each run, Pallas kernels for 0% -> 0%
where the time goes in v1:
time: 349 us; the launch traced here: 347 us
  waiting for transfers between devices  221 us (63%)
  matrix products  54.3 us (16%)
  local copies, waits for them, and re-layouts  27 us (8%)
  starting transfers between devices  20.9 us (6%)
  between operations  13.8 us (4%)
  other arithmetic  10.5 us (3%)
    ppermute x7, waiting for transfers between devices, body(): lax.ppermute(ring[-1], 'tensor', [(dev, (dev + 1) % 8) for dev in range(8)])  83.3 us
    reduce_scatter x1, waiting for transfers between devices, body(): lax.psum_scatter(terms.astype(jnp.bfloat16), 'tensor', scatter_dimension=...  52.8 us
    all_to_all x1, waiting for transfers between devices, sent_and_summed(): lax.all_to_all(parts, axis, split_axis=0, concat_axis=0, tiled=True)  34.9 us
    all_to_all x1, waiting for transfers between devices, from_everyone(): lax.all_to_all(jnp.broadcast_to(x[None], (devices, *x.shape)), axis, 0, 0...  33 us
    all_to_all x1, waiting for transfers between devices, body(): lax.all_to_all(outgoing, 'dp', split_axis=0, concat_axis=0, tiled=True)  17 us
    dot_general x1, matrix products, body(): terms = jnp.dot(hidden, down_full, preferred_element_type=jnp.float32)  15.8 us
    dot_general x1, matrix products, body(): upward = jnp.dot(normed_seq, up_full, preferred_element_type=jnp.float32)  14.2 us
    concatenate x1, local copies, waits for them, and re-layouts, body(): jnp.roll(jnp.concatenate(ring[::-1], axis=1), (lax.axis_index('tensor') +...  11.6 us
  transfers between devices with their start and end apart: 12, of which 11 were waited for; matrix products, arithmetic and copies ran while one was open for 14% of the time, Pallas kernels for 0%

profile of v1, /device:TPU:1, one launch (start us, length us, event | category | flops | bytes accessed | tf_op | source)
XLA Modules:
  0.0 347.4 jit_solution(16510061851415440405)
XLA Ops:
  6.5 0.0 all-gather.2.cloned.1.call-start
  6.6 2.4 concatenate.14
  9.0 0.0 all-gather.2.cloned.1.call-update
  9.0 0.3 fusion.13
  9.4 0.2 broadcast_compare_fusion
  9.6 1.7 convolution_convert_fusion.3
  11.3 1.7 convolution_convert_fusion.2
  12.9 1.0 fusion.54
  13.9 1.7 convolution_convert_fusion.4
  15.6 1.2 convolution_convert_fusion.1
  16.9 1.7 convolution_convert_fusion
  18.5 9.0 %all-to-all-start = ((bf16[8,64,1280]{2,1,0:T(8,128)(2,1)}), bf16[8,64,1280]{2,1,0:T(8,128)(2,1)S(1)}, u32[]{:S(2)}, u32[]{:S(2)}) async-start(bf16[8,64,1280]{2,1,0:T(8,128)(2,1)} %bitcast.15), calls=%async_computation | async-start | bytes 2621440 | tf_op jit(solution)/shard_map/all_to_all | solution.py:19
  27.5 34.9 %all-to-all-done = bf16[8,64,1280]{2,1,0:T(8,128)(2,1)S(1)} async-done(((bf16[8,64,1280]{2,1,0:T(8,128)(2,1)}), bf16[8,64,1280]{2,1,0:T(8,128)(2,1)S(1)}, u32[]{:S(2)}, u32[]{:S(2)}) %all-to-all-start) | async-done | bytes 1310752 | tf_op jit(solution)/shard_map/all_to_all | solution.py:19
  62.4 0.2 convert_reduce_fusion
  62.6 0.0 copy-start.4
  62.6 0.0 copy-start.6
  62.6 0.0 copy-start.3
  62.7 1.2 broadcast_in_dim.103
  63.9 3.6 %all-to-all-start.1 = ((bf16[8,64,1280]{2,1,0:T(8,128)(2,1)}), bf16[8,64,1280]{2,1,0:T(8,128)(2,1)S(1)}, u32[]{:S(2)}, u32[]{:S(2)}) async-start(bf16[8,64,1280]{2,1,0:T(8,128)(2,1)} %broadcast_in_dim.103), calls=%async_computation.1 | async-start | bytes 2621440 | tf_op jit(solution)/shard_map/all_to_all | solution.py:25
  67.5 0.1 copy.26
  67.6 0.1 reduce-window.8
  67.6 0.1 reduce.1
  67.8 0.1 add_select_fusion
  67.8 0.1 select_n.111
  67.9 0.1 constant_dynamic-slice_fusion.1
  68.0 0.1 copy.31
  68.1 0.2 copy.29
  68.3 0.7 fusion.37
  69.0 0.1 select_reduce_fusion.1
  69.1 0.1 iota_compare_fusion.2
  69.2 33.0 %all-to-all-done.1 = bf16[8,64,1280]{2,1,0:T(8,128)(2,1)S(1)} async-done(((bf16[8,64,1280]{2,1,0:T(8,128)(2,1)}), bf16[8,64,1280]{2,1,0:T(8,128)(2,1)S(1)}, u32[]{:S(2)}, u32[]{:S(2)}) %all-to-all-start.1) | async-done | bytes 1310752 | tf_op jit(solution)/shard_map/all_to_all | solution.py:25
  102.2 0.3 multiply_reduce_fusion
  102.5 0.1 rsqrt.29
  102.6 0.4 mul.100
  103.0 2.0 copy.32
  105.1 1.9 reshape.242
  107.0 5.2 %fusion.20 = bf16[128,448]{0,1:T(8,128)(2,1)S(1)} fusion(bf16[5120,448]{0,1:T(8,128)(2,1)} %param.20, f32[128,5120]{1,0:T(8,128)} %reshape.242, f32[128,5120]{1,0:T(8,128)} %bitcast.49, f32[5120]{0:T(1024)S(1)} %mul.104), kind=kOutput, calls=%fused_computation.36 | convolution fusion | flops 589225984 | bytes 9965568 | tf_op jit(solution)/shard_map/dot_general | solution.py:106
  112.2 0.1 copy.28
  112.3 0.1 pad_maximum_fusion
  112.4 4.0 %gather_fusion = bf16[1024,448]{1,0:T(8,128)(2,1)S(1)} fusion(bf16[512,448]{1,0:T(8,128)(2,1)S(1)} %pad_maximum_fusion, s32[1024]{0:T(1024)S(1)} %broadcast_clamp_fusion), kind=kCustom, calls=%fused_computation | custom fusion | bytes 1839104 | tf_op jit(solution)/shard_map/jit(_take)/gather | solution.py:117
  116.4 1.3 select_select_fusion
  117.6 7.8 %all-to-all-start.2 = ((bf16[32,32,448]{2,1,0:T(8,128)(2,1)}), bf16[32,32,448]{2,1,0:T(8,128)(2,1)S(1)}, u32[]{:S(2)}, u32[]{:S(2)}) async-start(bf16[32,32,448]{2,1,0:T(8,128)(2,1)} %select_select_fusion), calls=%async_computation.2 | async-start | bytes 2097152 | tf_op jit(solution)/shard_map/all_to_all | solution.py:119
  125.5 0.0 reduce-scatter.2.cloned.1.call-start
  125.5 0.1 select_reduce_fusion
  125.7 17.0 %all-to-all-done.2 = bf16[32,32,448]{2,1,0:T(8,128)(2,1)S(1)} async-done(((bf16[32,32,448]{2,1,0:T(8,128)(2,1)}), bf16[32,32,448]{2,1,0:T(8,128)(2,1)S(1)}, u32[]{:S(2)}, u32[]{:S(2)}) %all-to-all-start.2) | async-done | bytes 917536 | tf_op jit(solution)/shard_map/all_to_all | solution.py:119
  142.7 2.0 gather_fusion.1
  144.6 0.1 broadcast_select_fusion
  144.8 0.4 collective-permute-start
  145.1 14.0 %collective-permute-done = bf16[512,448]{1,0:T(8,128)(2,1)S(1)} collective-permute-done((bf16[512,448]{1,0:T(8,128)(2,1)S(1)}, bf16[512,448]{1,0:T(8,128)(2,1)S(1)}, u32[]{:S(2)}, u32[]{:S(2)}) %collective-permute-start) | collective-permute-done | bytes 458784 | tf_op jit(solution)/shard_map/ppermute | solution.py:134
  159.2 13.4 %collective-permute-done.1 = bf16[512,448]{1,0:T(8,128)(2,1)S(1)} collective-permute-done((bf16[512,448]{1,0:T(8,128)(2,1)S(1)}, bf16[512,448]{1,0:T(8,128)(2,1)S(1)}, u32[]{:S(2)}, u32[]{:S(2)}) %collective-permute-start.1) | collective-permute-done | bytes 458784 | tf_op jit(solution)/shard_map/ppermute | solution.py:134
  172.6 12.5 %collective-permute-done.2 = bf16[512,448]{1,0:T(8,128)(2,1)S(1)} collective-permute-done((bf16[512,448]{1,0:T(8,128)(2,1)S(1)}, bf16[512,448]{1,0:T(8,128)(2,1)S(1)}, u32[]{:S(2)}, u32[]{:S(2)}) %collective-permute-start.2) | collective-permute-done | bytes 458784 | tf_op jit(solution)/shard_map/ppermute | solution.py:134
  185.1 11.6 %collective-permute-done.3 = bf16[512,448]{1,0:T(8,128)(2,1)S(1)} collective-permute-done((bf16[512,448]{1,0:T(8,128)(2,1)S(1)}, bf16[512,448]{1,0:T(8,128)(2,1)S(1)}, u32[]{:S(2)}, u32[]{:S(2)}) %collective-permute-start.3) | collective-permute-done | bytes 458784 | tf_op jit(solution)/shard_map/ppermute | solution.py:134
  196.6 10.6 %collective-permute-done.4 = bf16[512,448]{1,0:T(8,128)(2,1)S(1)} collective-permute-done((bf16[512,448]{1,0:T(8,128)(2,1)S(1)}, bf16[512,448]{1,0:T(8,128)(2,1)S(1)}, u32[]{:S(2)}, u32[]{:S(2)}) %collective-permute-start.4) | collective-permute-done | bytes 458784 | tf_op jit(solution)/shard_map/ppermute | solution.py:134
  207.2 10.5 %collective-permute-done.5 = bf16[512,448]{1,0:T(8,128)(2,1)} collective-permute-done((bf16[512,448]{1,0:T(8,128)(2,1)S(1)}, bf16[512,448]{1,0:T(8,128)(2,1)}, u32[]{:S(2)}, u32[]{:S(2)}) %collective-permute-start.5) | collective-permute-done | bytes 458784 | tf_op jit(solution)/shard_map/ppermute | solution.py:134
  217.7 10.7 %collective-permute-done.6 = bf16[512,448]{1,0:T(8,128)(2,1)} collective-permute-done((bf16[512,448]{1,0:T(8,128)(2,1)}, bf16[512,448]{1,0:T(8,128)(2,1)}, u32[]{:S(2)}, u32[]{:S(2)}) %collective-permute-start.6) | collective-permute-done | bytes 458784 | tf_op jit(solution)/shard_map/ppermute | solution.py:134
  228.4 11.6 %concatenate.13 = bf16[512,7168]{1,0:T(8,128)(2,1)} concatenate(bf16[512,448]{1,0:T(8,128)(2,1)} %collective-permute-done.6, bf16[512,448]{1,0:T(8,128)(2,1)} %collective-permute-done.5, bf16[512,448]{1,0:T(8,128)(2,1)S(1)} %collective-permute-done.4, bf16[512,448]{1,0:T(8,128)(2,1)S(1)} %collective-permute-done.3, bf16[512,448]{1,0:T(8,128)(2,1)S(1)} %collective-permute-done.2, ...), dimensions={1} | concatenate | bytes 14680064 | tf_op jit(solution)/shard_map/jit(_roll_dynamic)/concatenate | solution.py:135
  240.0 5.2 %fusion.7 = f32[512]{0:T(512)S(1)} fusion(bf16[512,7168]{1,0:T(8,128)(2,1)} %concatenate.13, s32[]{:T(128)S(6)} %select_n.119), kind=kLoop, calls=%fused_computation.11 | loop fusion | flops 5504512 | bytes 3672068 | tf_op jit(solution)/shard_map/reduce_sum | solution.py:55
  245.2 0.0 all-gather.2.cloned.1.call-done
  245.3 14.2 %fusion.3 = f32[512,1184]{0,1:T(8,128)S(1)} fusion(bf16[3584,3552]{1,0:T(8,128)(2,1)} %all-gather.2.cloned.1.call-done, f32[3584]{0:T(1024)S(1)} %copy-done.7, f32[512]{0:T(512)S(1)} %add_rsqrt_fusion.1, bf16[512,7168]{1,0:T(8,128)(2,1)} %concatenate.13, s32[]{:T(128)S(6)} %select_n.119), kind=kOutput, calls=%fused_computation.5 | convolution fusion | flops 4352638976 | bytes 15286276 | tf_op jit(solution)/shard_map/dot_general | solution.py:145
  259.5 10.2 %fusion.5 = f32[512,1184]{0,1:T(8,128)S(1)} fusion(bf16[3584,3552]{1,0:T(8,128)(2,1)} %all-gather.2.cloned.1.call-done, f32[3584]{0:T(1024)S(1)} %copy-done.7, f32[512]{0:T(512)S(1)} %add_rsqrt_fusion.1, bf16[512,7168]{1,0:T(8,128)(2,1)} %concatenate.13, s32[]{:T(128)S(6)} %select_n.119), kind=kOutput, calls=%fused_computation.7 | convolution fusion | flops 4352638976 | bytes 15286276 | tf_op jit(solution)/shard_map/dot_general | solution.py:144
  269.7 15.8 %fusion.10 = bf16[512,3584]{1,0:T(8,128)(2,1)} fusion(bf16[3584,3552]{1,0:T(8,128)(2,1)} %all-gather.2.cloned.1.call-done, f32[512,1184]{0,1:T(8,128)S(1)} %fusion.3, f32[512,1184]{0,1:T(8,128)S(1)} %fusion.5), kind=kOutput, calls=%fused_computation.14 | convolution fusion | flops 4350771200 | bytes 17694720 | tf_op jit(solution)/shard_map/dot_general | solution.py:147
  285.5 0.0 reduce-scatter.2.cloned.1.call-update
  285.6 52.8 %reduce-scatter.2.cloned.1.call-done = bf16[64,3584]{1,0:T(8,128)(2,1)} async-done(((bf16[512,3584]{1,0:T(8,128)(2,1)}), bf16[64,3584]{1,0:T(8,128)(2,1)}) %reduce-scatter.2.cloned.1.call-update) | async-done | bytes 458768 | tf_op jit(solution)/shard_map/reduce_scatter | solution.py:148
  338.4 2.2 add_convert_fusion
  (36 shorter events, 0.2 us)
Async XLA Ops:
  6.5 10.3 %copy-start = (bf16[160,1280]{1,0:T(8,128)(2,1)S(1)}, bf16[160,1280]{1,0:T(8,128)(2,1)}, u32[]{:S(2)}) copy-start(bf16[160,1280]{1,0:T(8,128)(2,1)} %param.18) | copy-start | bytes 1228804
  6.5 2.5 copy-start.2
  6.5 2.8 copy-start.5
  6.5 3.1 copy-start.8
  6.5 238.7 %all-gather.2.cloned.1.call-start = ((), (), s32[]{:S(2)}) async-start(), calls=%async_computation.4 | async-start | bytes 26492928 | tf_op jit(solution)/shard_map/all_gather | solution.py:43
  18.5 43.9 %all-to-all-start = ((bf16[8,64,1280]{2,1,0:T(8,128)(2,1)}), bf16[8,64,1280]{2,1,0:T(8,128)(2,1)S(1)}, u32[]{:S(2)}, u32[]{:S(2)}) async-start(bf16[8,64,1280]{2,1,0:T(8,128)(2,1)} %bitcast.15), calls=%async_computation | async-start | bytes 2621440 | tf_op jit(solution)/shard_map/all_to_all | solution.py:19
  62.6 4.9 %copy-start.4 = (s32[32,32]{1,0:T(8,128)S(1)}, s32[32,32]{1,0:T(8,128)}, u32[]{:S(2)}) copy-start(s32[32,32]{1,0:T(8,128)} %param.22) | copy-start | bytes 12292
  62.6 5.5 %copy-start.6 = (f32[1280]{0:T(1024)S(1)}, f32[1280]{0:T(1024)}, u32[]{:S(2)}) copy-start(f32[1280]{0:T(1024)} %param.19) | copy-start | bytes 15364
  62.6 5.5 %copy-start.3 = (bf16[384,448]{0,1:T(8,128)(2,1)S(1)}, bf16[384,448]{0,1:T(8,128)(2,1)}, u32[]{:S(2)}) copy-start(bf16[384,448]{0,1:T(8,128)(2,1)} %param.21) | copy-start | bytes 1032196
  63.9 38.3 %all-to-all-start.1 = ((bf16[8,64,1280]{2,1,0:T(8,128)(2,1)}), bf16[8,64,1280]{2,1,0:T(8,128)(2,1)S(1)}, u32[]{:S(2)}, u32[]{:S(2)}) async-start(bf16[8,64,1280]{2,1,0:T(8,128)(2,1)} %broadcast_in_dim.103), calls=%async_computation.1 | async-start | bytes 2621440 | tf_op jit(solution)/shard_map/all_to_all | solution.py:25
  117.6 25.0 %all-to-all-start.2 = ((bf16[32,32,448]{2,1,0:T(8,128)(2,1)}), bf16[32,32,448]{2,1,0:T(8,128)(2,1)S(1)}, u32[]{:S(2)}, u32[]{:S(2)}) async-start(bf16[32,32,448]{2,1,0:T(8,128)(2,1)} %select_select_fusion), calls=%async_computation.2 | async-start | bytes 2097152 | tf_op jit(solution)/shard_map/all_to_all | solution.py:119
  125.5 212.9 %reduce-scatter.2.cloned.1.call-start = ((), (), s32[]{:S(2)}) async-start(), calls=%async_computation.5 | async-start | bytes 4128768 | tf_op jit(solution)/shard_map/reduce_scatter | solution.py:148
  144.8 14.4 %collective-permute-start = (bf16[512,448]{1,0:T(8,128)(2,1)S(1)}, bf16[512,448]{1,0:T(8,128)(2,1)S(1)}, u32[]{:S(2)}, u32[]{:S(2)}) collective-permute-start(bf16[512,448]{1,0:T(8,128)(2,1)S(1)} %broadcast_select_fusion), channel_id=1, source_target_pairs={{0,1},{1,2},{2,3},{3,4},{4,5},{5,6},{6,7},{7,0},{8,9},{9,10},{10,1... | collective-permute-start | bytes 1376264 | tf_op jit(solution)/shard_map/ppermute | solution.py:134
  159.2 13.4 %collective-permute-start.1 = (bf16[512,448]{1,0:T(8,128)(2,1)S(1)}, bf16[512,448]{1,0:T(8,128)(2,1)S(1)}, u32[]{:S(2)}, u32[]{:S(2)}) collective-permute-start(bf16[512,448]{1,0:T(8,128)(2,1)S(1)} %collective-permute-done), channel_id=1, source_target_pairs={{0,1},{1,2},{2,3},{3,4},{4,5},{5,6},{6,7},{7,0},{8,9},{9,10},{10,1... | collective-permute-start | bytes 1376264 | tf_op jit(solution)/shard_map/ppermute | solution.py:134
  172.6 12.5 %collective-permute-start.2 = (bf16[512,448]{1,0:T(8,128)(2,1)S(1)}, bf16[512,448]{1,0:T(8,128)(2,1)S(1)}, u32[]{:S(2)}, u32[]{:S(2)}) collective-permute-start(bf16[512,448]{1,0:T(8,128)(2,1)S(1)} %collective-permute-done.1), channel_id=1, source_target_pairs={{0,1},{1,2},{2,3},{3,4},{4,5},{5,6},{6,7},{7,0},{8,9},{9,10},{10,1... | collective-permute-start | bytes 1376264 | tf_op jit(solution)/shard_map/ppermute | solution.py:134
  185.1 11.6 %collective-permute-start.3 = (bf16[512,448]{1,0:T(8,128)(2,1)S(1)}, bf16[512,448]{1,0:T(8,128)(2,1)S(1)}, u32[]{:S(2)}, u32[]{:S(2)}) collective-permute-start(bf16[512,448]{1,0:T(8,128)(2,1)S(1)} %collective-permute-done.2), channel_id=1, source_target_pairs={{0,1},{1,2},{2,3},{3,4},{4,5},{5,6},{6,7},{7,0},{8,9},{9,10},{10,1... | collective-permute-start | bytes 1376264 | tf_op jit(solution)/shard_map/ppermute | solution.py:134
  196.6 10.6 %collective-permute-start.4 = (bf16[512,448]{1,0:T(8,128)(2,1)S(1)}, bf16[512,448]{1,0:T(8,128)(2,1)S(1)}, u32[]{:S(2)}, u32[]{:S(2)}) collective-permute-start(bf16[512,448]{1,0:T(8,128)(2,1)S(1)} %collective-permute-done.3), channel_id=1, source_target_pairs={{0,1},{1,2},{2,3},{3,4},{4,5},{5,6},{6,7},{7,0},{8,9},{9,10},{10,1... | collective-permute-start | bytes 1376264 | tf_op jit(solution)/shard_map/ppermute | solution.py:134
  207.2 10.5 %collective-permute-start.5 = (bf16[512,448]{1,0:T(8,128)(2,1)S(1)}, bf16[512,448]{1,0:T(8,128)(2,1)}, u32[]{:S(2)}, u32[]{:S(2)}) collective-permute-start(bf16[512,448]{1,0:T(8,128)(2,1)S(1)} %collective-permute-done.4), channel_id=1, source_target_pairs={{0,1},{1,2},{2,3},{3,4},{4,5},{5,6},{6,7},{7,0},{8,9},{9,10},{10,1... | collective-permute-start | bytes 1376264 | tf_op jit(solution)/shard_map/ppermute | solution.py:134
  217.7 10.7 %collective-permute-start.6 = (bf16[512,448]{1,0:T(8,128)(2,1)}, bf16[512,448]{1,0:T(8,128)(2,1)}, u32[]{:S(2)}, u32[]{:S(2)}) collective-permute-start(bf16[512,448]{1,0:T(8,128)(2,1)} %collective-permute-done.5), channel_id=1, source_target_pairs={{0,1},{1,2},{2,3},{3,4},{4,5},{5,6},{6,7},{7,0},{8,9},{9,10},{10,1... | collective-permute-start | bytes 1376264 | tf_op jit(solution)/shard_map/ppermute | solution.py:134
  240.0 5.3 %copy-start.7 = (f32[3584]{0:T(1024)S(1)}, f32[3584]{0:T(1024)}, u32[]{:S(2)}) copy-start(f32[3584]{0:T(1024)} %param.24) | copy-start | bytes 43012
  269.7 70.9 %copy-start.1 = (bf16[160,1280]{1,0:T(8,128)(2,1)S(1)}, bf16[160,1280]{1,0:T(8,128)(2,1)}, u32[]{:S(2)}) copy-start(bf16[160,1280]{1,0:T(8,128)(2,1)} %param.18) | copy-start | bytes 1228804
Sparse Core Ops, SparseCore 0:
  9.9 102.6 all-gather.1
  285.7 52.6 reduce-scatter.1
